TPU v7x, 128 devices: a whole 4x4x4 slice. The times are simulated.
128 devices in a mesh: row: 8 (over y, core), col: 16 (over x, z).
Axes of the slice: x: 4, y: 4, z: 4, core: 2. Of those that a mesh axis runs over, the one named last changes fastest.
Arguments:
- b_tensor: bfloat16 [128, 1024, 1024], P('col', 'row'), may hold values from -6 to 6
- occ_green: bfloat16 [1024, 1024], P(('row', 'col')), may hold values from -0.1875 to 0.1875
- virt_green: bfloat16 [1024, 1024], P(('row', 'col')), may hold values from -0.1875 to 0.1875
- b_mask: int32 [1, 8, 8], replicated, may hold values 0 or 1
- occ_mask: int32 [8, 8], replicated, may hold values 0 or 1
- virt_mask: int32 [8, 8], replicated, may hold values 0 or 1
Outputs:
- chi: float32 [128, 128], P(('row', 'col'))
All inputs are finite; a program needn't handle non-finite values.
Results may differ from a plain program's by a relative error of at most 0.0041.
Values may be sent and summed in bfloat16 or wider, within the bound.
A program may use at most 64 MiB of HBM per device.

v0:
```python
import jax
import jax.numpy as jnp
from jax import lax
from jax.sharding import PartitionSpec as P

TILE = 128


def expand_pair(mask):
    return jnp.repeat(jnp.repeat(mask, TILE, axis=0), TILE, axis=1).astype(jnp.bfloat16)


def per_device(b_tensor, occ_green, virt_green, b_mask, occ_mask, virt_mask):
    col_index = lax.axis_index("col")
    row_index = lax.axis_index("row")
    p_count, m_count, n_basis = b_tensor.shape
    p_tiles = (col_index * p_count + jnp.arange(p_count, dtype=jnp.int32)) // TILE
    m_tiles = (row_index * m_count + jnp.arange(m_count, dtype=jnp.int32)) // TILE
    local_mask = jnp.take(jnp.take(b_mask, p_tiles, axis=0), m_tiles, axis=1).astype(jnp.bfloat16)
    masked = b_tensor * jnp.repeat(local_mask, TILE, axis=2)
    exchanged_b = lax.all_to_all(masked, "col", split_axis=2, concat_axis=0, tiled=True)
    virt_full = lax.all_gather(virt_green, ("row", "col"), axis=0, tiled=True) * expand_pair(
        virt_mask
    )
    occ_rows = lax.all_gather(occ_green, "col", axis=0, tiled=True)
    occ_rows = occ_rows * lax.dynamic_slice_in_dim(
        expand_pair(occ_mask), row_index * m_count, m_count, 0
    )
    inner = jnp.dot(masked.reshape(-1, n_basis), virt_full, preferred_element_type=jnp.float32)
    inner = inner.astype(jnp.bfloat16).reshape(masked.shape)
    outer = jnp.einsum(
        "lm,pms->pls",
        occ_rows,
        lax.all_gather(inner, "row", axis=1, tiled=True),
        preferred_element_type=jnp.float32,
    ).astype(jnp.bfloat16)
    moved = lax.all_to_all(outer, "col", split_axis=2, concat_axis=0, tiled=True)
    b_flat = exchanged_b.reshape(exchanged_b.shape[0], -1)
    y_flat = moved.reshape(moved.shape[0], -1)
    summed = lax.psum_scatter(
        lax.dot_general(
            y_flat, b_flat, (((1,), (1,)), ((), ())), preferred_element_type=jnp.float32
        ),
        ("row", "col"),
        scatter_dimension=0,
        tiled=True,
    )
    return summed * (-2.0 / n_basis)


def solution(mesh):
    return jax.shard_map(
        per_device,
        mesh=mesh,
        in_specs=(
            P("col", "row", None),
            P(("row", "col"), None),
            P(("row", "col"), None),
            P(),
            P(),
            P(),
        ),
        out_specs=P(("row", "col"), None),
        check_vma=False,
    )
```

profile of v0, /device:TPU:1, one launch (start us, length us, event | category | flops | bytes accessed | tf_op | source)
XLA Modules:
  0.0 387.0 jit_solution(18253904898014795396)
XLA Ops:
  9.2 1.4 broadcast_in_dim.39
  10.5 2.3 reshape.157
  12.8 3.2 mul.24
  16.1 63.1 %all-gather.3.cloned.1.call-done = bf16[1024,1024]{1,0:T(8,128)(2,1)} async-done(((bf16[8,1024]{1,0:T(8,128)(2,1)}), bf16[1024,1024]{1,0:T(8,128)(2,1)}) %all-gather.3.cloned.1.call-update) | async-done | bytes 2097168 | tf_op jit(solution)/shard_map/all_gather | solution.py:22
  79.3 2.9 broadcast_in_dim.41
  82.2 3.7 fusion.2
  85.9 3.9 %copy.19 = bf16[8,128,1024]{1,2,0:T(8,128)(2,1)} copy(bf16[8,128,1024]{2,1,0:T(8,128)(2,1)} %bitcast.45) | data formatting | bytes 4194304 | tf_op jit(solution)/shard_map/reshape | solution.py:30
  89.9 2.9 copy.22
  92.8 4.2 %all-to-all-start.1 = ((bf16[8,128,1024]{1,0,2:T(8,128)(2,1)}), bf16[8,128,1024]{1,0,2:T(8,128)(2,1)S(1)}, u32[]{:S(2)}, u32[]{:S(2)}) async-start(bf16[8,128,1024]{1,0,2:T(8,128)(2,1)} %copy.22), calls=%async_computation.1 | async-start | bytes 4194304 | tf_op jit(solution)/shard_map/all_to_all | solution.py:21
  97.1 2.9 broadcast_in_dim.43
  100.1 2.0 copy.35
  102.0 36.4 %all_gather.11 = bf16[128,1024]{1,0:T(8,128)(2,1)S(1)} all-gather(bf16[8,1024]{1,0:T(8,128)(2,1)S(1)} %copy-done), channel_id=1, replica_groups=mesh['row'=8,'col'=16] {'col'}, dimensions={0}, use_global_device_ids=true | all-gather | bytes 278528 | tf_op jit(solution)/shard_map/all_gather | solution.py:25
  138.5 39.3 %all-gather.5.cloned.1.call-done = bf16[8,1024,1024]{1,2,0:T(8,128)(2,1)} async-done(((bf16[8,128,1024]{1,2,0:T(8,128)(2,1)}), bf16[8,1024,1024]{1,2,0:T(8,128)(2,1)}) %all-gather.5.cloned.1.call-update) | async-done | bytes 16777232 | tf_op jit(solution)/shard_map/all_gather | solution.py:34
  177.7 10.3 %convert_bitcast_fusion = bf16[8,128,1024]{1,2,0:T(8,128)(2,1)S(1)} fusion(bf16[8,1024,1024]{1,2,0:T(8,128)(2,1)} %all-gather.5.cloned.1.call-done, bf16[128,1024]{1,0:T(8,128)(2,1)S(1)} %all_gather.11, bf16[1024,1024]{1,0:T(8,128)(2,1)} %bitcast.44, s32[]{:T(128)S(6)} %select_n.83), kind=kOutput, calls=%fused_computation.5 | convolution fusion | flops 2149056512 | bytes 19398660 | tf_op jit(solution)/shard_map/lm,pms->pls/dot_general | solution.py:31
  188.0 2.7 copy.20
  190.7 6.7 %all-to-all-start = ((bf16[8,128,1024]{1,0,2:T(8,128)(2,1)}), bf16[8,128,1024]{1,0,2:T(8,128)(2,1)}, u32[]{:S(2)}, u32[]{:S(2)}) async-start(bf16[8,128,1024]{1,0,2:T(8,128)(2,1)} %copy.20), calls=%async_computation | async-start | bytes 4194304 | tf_op jit(solution)/shard_map/all_to_all | solution.py:37
  197.5 3.2 copy.24
  200.7 5.7 %reshape.161 = bf16[128,8192]{1,0:T(8,128)(2,1)S(1)} reshape(bf16[16,8,128,64]{3,2,1,0:T(8,128)(2,1)} %copy.24) | data formatting | bytes 4194304 | tf_op jit(solution)/shard_map/reshape | solution.py:38
  206.4 20.3 %all-to-all-done = bf16[8,128,1024]{1,0,2:T(8,128)(2,1)} async-done(((bf16[8,128,1024]{1,0,2:T(8,128)(2,1)}), bf16[8,128,1024]{1,0,2:T(8,128)(2,1)}, u32[]{:S(2)}, u32[]{:S(2)}) %all-to-all-start) | async-done | bytes 2097184 | tf_op jit(solution)/shard_map/all_to_all | solution.py:37
  226.7 4.8 %copy.21 = bf16[8,128,16,64]{3,1,0,2:T(8,128)(2,1)} copy(bf16[8,128,16,64]{1,0,3,2:T(8,128)(2,1)} %bitcast.9) | data formatting | bytes 4194304 | tf_op jit(solution)/shard_map/all_to_all | solution.py:37
  231.5 6.6 %reshape.160 = bf16[128,8192]{1,0:T(8,128)(2,1)} reshape(bf16[16,8,128,64]{3,2,1,0:T(8,128)(2,1)} %bitcast.39) | data formatting | bytes 4194304 | tf_op jit(solution)/shard_map/reshape | solution.py:39
  238.1 2.9 fusion.9
  241.1 138.1 %all-reduce.3.cloned.1.call-done = f32[128,128]{1,0:T(8,128)} async-done(((f32[128,128]{1,0:T(8,128)}), f32[128,128]{1,0:T(8,128)}) %all-reduce.3.cloned.1.call-update) | async-done | bytes 65552
  379.2 1.2 dynamic-slice_multiply_fusion
  (27 shorter events, 2.7 us)
Async XLA Ops:
  6.5 72.7 %all-gather.3.cloned.1.call-start = ((), (), s32[]{:S(2)}) async-start(), calls=%async_computation.2 | async-start | bytes 2113536 | tf_op jit(solution)/shard_map/all_gather | solution.py:22
  7.3 170.5 %all-gather.5.cloned.1.call-start = ((), (), s32[]{:S(2)}) async-start(), calls=%async_computation.3 | async-start | bytes 18874368 | tf_op jit(solution)/shard_map/all_gather | solution.py:34
  10.5 2.3 copy-start.1
  79.2 3.0 copy-start.3
  92.8 4.2 %copy-start.2 = (s32[8,8]{1,0:T(8,128)S(1)}, s32[8,8]{1,0:T(8,128)}, u32[]{:S(2)}) copy-start(s32[8,8]{1,0:T(8,128)} %param.10) | copy-start | bytes 772
  92.8 97.9 %all-to-all-start.1 = ((bf16[8,128,1024]{1,0,2:T(8,128)(2,1)}), bf16[8,128,1024]{1,0,2:T(8,128)(2,1)S(1)}, u32[]{:S(2)}, u32[]{:S(2)}) async-start(bf16[8,128,1024]{1,0,2:T(8,128)(2,1)} %copy.22), calls=%async_computation.1 | async-start | bytes 4194304 | tf_op jit(solution)/shard_map/all_to_all | solution.py:21
  100.0 2.0 copy-start
  190.7 36.0 %all-to-all-start = ((bf16[8,128,1024]{1,0,2:T(8,128)(2,1)}), bf16[8,128,1024]{1,0,2:T(8,128)(2,1)}, u32[]{:S(2)}, u32[]{:S(2)}) async-start(bf16[8,128,1024]{1,0,2:T(8,128)(2,1)} %copy.20), calls=%async_computation | async-start | bytes 4194304 | tf_op jit(solution)/shard_map/all_to_all | solution.py:37
  197.5 181.8 %all-reduce.3.cloned.1.call-start = ((), (), s32[]{:S(2)}) async-start(), calls=%async_computation.4 | async-start | bytes 131072
Sparse Core Ops, SparseCore 0:
  10.3 68.8 all-gather.2
  90.0 87.6 all-gather.4
  241.2 137.9 all-reduce.2
where the time goes:
time: 388 us; the launch traced here: 387 us
  waiting for transfers between devices  262 us (68%)
  local copies, waits for them, and re-layouts  42.2 us (11%)
  blocking collectives  36.4 us (9%)
  matrix products  16.9 us (4%)
  between operations  13.3 us (3%)
  starting transfers between devices  11 us (3%)
  other arithmetic  5.47 us (1%)
    unnamed x4, waiting for transfers between devices  139 us
    all_gather x1, waiting for transfers between devices, per_device(): lax.all_gather(virt_green, ('row', 'col'), axis=0, tiled=True)  63.1 us
    all_gather x1, waiting for transfers between devices, per_device(): lax.all_gather(inner, 'row', axis=1, tiled=True)  39.3 us
    all_gather x1, blocking collectives, per_device(): occ_rows = lax.all_gather(occ_green, 'col', axis=0, tiled=True)  36.4 us
    all_to_all x1, waiting for transfers between devices, per_device(): lax.all_to_all(outer, 'col', split_axis=2, concat_axis=0, tiled=True)  20.3 us
    dot_general x1, matrix products, per_device(): jnp.einsum('lm,pms->pls', occ_rows, lax.all_gather(inner, 'row', axis=1,...  10.3 us
  transfers between devices with their start and end apart: 5, of which 4 were waited for; matrix products, arithmetic and copies ran while one was open for 10% of the time, Pallas kernels for 0%

commit v1 on v0

--- a/solution.py
+++ b/solution.py
@@ -22,7 +22,13 @@
     virt_full = lax.all_gather(virt_green, ("row", "col"), axis=0, tiled=True) * expand_pair(
         virt_mask
     )
-    occ_rows = lax.all_gather(occ_green, "col", axis=0, tiled=True)
+    n_dev = lax.axis_size("col")
+    held, blocks = (occ_green, [occ_green])
+    for _ in range(n_dev - 1):
+        held = lax.ppermute(held, "col", [(i, (i + 1) % n_dev) for i in range(n_dev)])
+        blocks.insert(0, held)
+    line = jnp.concatenate(blocks, axis=0)
+    occ_rows = jnp.roll(line, (lax.axis_index("col") + 1) * occ_green.shape[0], axis=0)
     occ_rows = occ_rows * lax.dynamic_slice_in_dim(
         expand_pair(occ_mask), row_index * m_count, m_count, 0
     )

time: 388 us -> 403 us (1.039)
  waiting for transfers between devices: 262 us -> 311 us
  blocking collectives: 36.4 us -> 0 us
    ppermute x0 -> x15, waiting for transfers between devices: none -> 82.7 us  [per_device(): lax.ppermute(held, 'col', [(i, (i + 1) % n_dev) for i in range(n_dev)])]
    all_gather x1, waiting for transfers between devices: 39.3 us -> 0.02 us  [per_device(): lax.all_gather(inner, 'row', axis=1, tiled=True)]
    all_gather x1 -> x0, blocking collectives: 36.4 us -> none  [per_device(): occ_rows = lax.all_gather(occ_green, 'col', axis=0, tiled=True)]
    unnamed x4, waiting for transfers between devices: 139 us -> 153 us
    all_to_all x1, waiting for transfers between devices: 20.3 us -> 12.2 us  [per_device(): lax.all_to_all(outer, 'col', split_axis=2, concat_axis=0, tiled=True)]
  transfers between devices with their start and end apart: 5 -> 20, of which waited for: 4 -> 17; matrix products, arithmetic and copies ran while one was open for 10% -> 10% of each run, Pallas kernels for 0% -> 0%
where the time goes in v1:
time: 403 us
  waiting for transfers between devices  311 us (77%)
  local copies, waits for them, and re-layouts  43 us (11%)
  matrix products  16.9 us (4%)
  between operations  13.6 us (3%)
  starting transfers between devices  13.1 us (3%)
  other arithmetic  5.47 us (1%)
    unnamed x4, waiting for transfers between devices  153 us
    ppermute x15, waiting for transfers between devices, per_device(): lax.ppermute(held, 'col', [(i, (i + 1) % n_dev) for i in range(n_dev)])  82.7 us
    all_gather x1, waiting for transfers between devices, per_device(): lax.all_gather(virt_green, ('row', 'col'), axis=0, tiled=True)  63.1 us
    all_to_all x1, waiting for transfers between devices, per_device(): lax.all_to_all(outer, 'col', split_axis=2, concat_axis=0, tiled=True)  12.2 us
    dot_general x1, matrix products, per_device(): jnp.einsum('lm,pms->pls', occ_rows, lax.all_gather(inner, 'row', axis=1,...  10.3 us
  transfers between devices with their start and end apart: 20, of which 17 were waited for; matrix products, arithmetic and copies ran while one was open for 10% of the time, Pallas kernels for 0%

profile of v1, /device:TPU:1, one launch (start us, length us, event | category | flops | bytes accessed | tf_op | source)
XLA Modules:
  0.0 402.8 jit_solution(12785328611807869072)
XLA Ops:
  16.1 63.1 %all-gather.3.cloned.1.call-done = bf16[1024,1024]{1,0:T(8,128)(2,1)} async-done(((bf16[8,1024]{1,0:T(8,128)(2,1)}), bf16[1024,1024]{1,0:T(8,128)(2,1)}) %all-gather.3.cloned.1.call-update) | async-done | bytes 2097168 | tf_op jit(solution)/shard_map/all_gather | solution.py:22
  85.9 3.9 copy.19
  90.6 5.9 %collective-permute-done = bf16[8,1024]{1,0:T(8,128)(2,1)S(1)} collective-permute-done((bf16[8,1024]{1,0:T(8,128)(2,1)S(1)}, bf16[8,1024]{1,0:T(8,128)(2,1)S(1)}, u32[]{:S(2)}, u32[]{:S(2)}) %collective-permute-start) | collective-permute-done | bytes 16416 | tf_op jit(solution)/shard_map/ppermute | solution.py:28
  96.5 5.9 %collective-permute-done.1 = bf16[8,1024]{1,0:T(8,128)(2,1)S(1)} collective-permute-done((bf16[8,1024]{1,0:T(8,128)(2,1)S(1)}, bf16[8,1024]{1,0:T(8,128)(2,1)S(1)}, u32[]{:S(2)}, u32[]{:S(2)}) %collective-permute-start.1) | collective-permute-done | bytes 16416 | tf_op jit(solution)/shard_map/ppermute | solution.py:28
  102.4 5.9 %collective-permute-done.2 = bf16[8,1024]{1,0:T(8,128)(2,1)S(1)} collective-permute-done((bf16[8,1024]{1,0:T(8,128)(2,1)S(1)}, bf16[8,1024]{1,0:T(8,128)(2,1)S(1)}, u32[]{:S(2)}, u32[]{:S(2)}) %collective-permute-start.2) | collective-permute-done | bytes 16416 | tf_op jit(solution)/shard_map/ppermute | solution.py:28
  108.3 5.9 %collective-permute-done.3 = bf16[8,1024]{1,0:T(8,128)(2,1)S(1)} collective-permute-done((bf16[8,1024]{1,0:T(8,128)(2,1)S(1)}, bf16[8,1024]{1,0:T(8,128)(2,1)S(1)}, u32[]{:S(2)}, u32[]{:S(2)}) %collective-permute-start.3) | collective-permute-done | bytes 16416 | tf_op jit(solution)/shard_map/ppermute | solution.py:28
  114.2 5.9 %collective-permute-done.4 = bf16[8,1024]{1,0:T(8,128)(2,1)S(1)} collective-permute-done((bf16[8,1024]{1,0:T(8,128)(2,1)S(1)}, bf16[8,1024]{1,0:T(8,128)(2,1)S(1)}, u32[]{:S(2)}, u32[]{:S(2)}) %collective-permute-start.4) | collective-permute-done | bytes 16416 | tf_op jit(solution)/shard_map/ppermute | solution.py:28
  120.1 5.9 %collective-permute-done.5 = bf16[8,1024]{1,0:T(8,128)(2,1)S(1)} collective-permute-done((bf16[8,1024]{1,0:T(8,128)(2,1)S(1)}, bf16[8,1024]{1,0:T(8,128)(2,1)S(1)}, u32[]{:S(2)}, u32[]{:S(2)}) %collective-permute-start.5) | collective-permute-done | bytes 16416 | tf_op jit(solution)/shard_map/ppermute | solution.py:28
  126.0 5.9 %collective-permute-done.6 = bf16[8,1024]{1,0:T(8,128)(2,1)S(1)} collective-permute-done((bf16[8,1024]{1,0:T(8,128)(2,1)S(1)}, bf16[8,1024]{1,0:T(8,128)(2,1)S(1)}, u32[]{:S(2)}, u32[]{:S(2)}) %collective-permute-start.6) | collective-permute-done | bytes 16416 | tf_op jit(solution)/shard_map/ppermute | solution.py:28
  131.9 5.9 %collective-permute-done.7 = bf16[8,1024]{1,0:T(8,128)(2,1)S(1)} collective-permute-done((bf16[8,1024]{1,0:T(8,128)(2,1)S(1)}, bf16[8,1024]{1,0:T(8,128)(2,1)S(1)}, u32[]{:S(2)}, u32[]{:S(2)}) %collective-permute-start.7) | collective-permute-done | bytes 16416 | tf_op jit(solution)/shard_map/ppermute | solution.py:28
  137.8 5.9 %collective-permute-done.8 = bf16[8,1024]{1,0:T(8,128)(2,1)S(1)} collective-permute-done((bf16[8,1024]{1,0:T(8,128)(2,1)S(1)}, bf16[8,1024]{1,0:T(8,128)(2,1)S(1)}, u32[]{:S(2)}, u32[]{:S(2)}) %collective-permute-start.8) | collective-permute-done | bytes 16416 | tf_op jit(solution)/shard_map/ppermute | solution.py:28
  143.8 5.9 %collective-permute-done.9 = bf16[8,1024]{1,0:T(8,128)(2,1)S(1)} collective-permute-done((bf16[8,1024]{1,0:T(8,128)(2,1)S(1)}, bf16[8,1024]{1,0:T(8,128)(2,1)S(1)}, u32[]{:S(2)}, u32[]{:S(2)}) %collective-permute-start.9) | collective-permute-done | bytes 16416 | tf_op jit(solution)/shard_map/ppermute | solution.py:28
  149.7 5.9 %collective-permute-done.10 = bf16[8,1024]{1,0:T(8,128)(2,1)S(1)} collective-permute-done((bf16[8,1024]{1,0:T(8,128)(2,1)S(1)}, bf16[8,1024]{1,0:T(8,128)(2,1)S(1)}, u32[]{:S(2)}, u32[]{:S(2)}) %collective-permute-start.10) | collective-permute-done | bytes 16416 | tf_op jit(solution)/shard_map/ppermute | solution.py:28
  155.6 5.9 %collective-permute-done.11 = bf16[8,1024]{1,0:T(8,128)(2,1)S(1)} collective-permute-done((bf16[8,1024]{1,0:T(8,128)(2,1)S(1)}, bf16[8,1024]{1,0:T(8,128)(2,1)S(1)}, u32[]{:S(2)}, u32[]{:S(2)}) %collective-permute-start.11) | collective-permute-done | bytes 16416 | tf_op jit(solution)/shard_map/ppermute | solution.py:28
  161.5 5.9 %collective-permute-done.12 = bf16[8,1024]{1,0:T(8,128)(2,1)S(1)} collective-permute-done((bf16[8,1024]{1,0:T(8,128)(2,1)S(1)}, bf16[8,1024]{1,0:T(8,128)(2,1)S(1)}, u32[]{:S(2)}, u32[]{:S(2)}) %collective-permute-start.12) | collective-permute-done | bytes 16416 | tf_op jit(solution)/shard_map/ppermute | solution.py:28
  167.4 5.9 %collective-permute-done.13 = bf16[8,1024]{1,0:T(8,128)(2,1)S(1)} collective-permute-done((bf16[8,1024]{1,0:T(8,128)(2,1)S(1)}, bf16[8,1024]{1,0:T(8,128)(2,1)S(1)}, u32[]{:S(2)}, u32[]{:S(2)}) %collective-permute-start.13) | collective-permute-done | bytes 16416 | tf_op jit(solution)/shard_map/ppermute | solution.py:28
  176.2 6.3 %all-to-all-start.1 = ((bf16[8,128,1024]{1,0,2:T(8,128)(2,1)}), bf16[8,128,1024]{1,0,2:T(8,128)(2,1)S(1)}, u32[]{:S(2)}, u32[]{:S(2)}) async-start(bf16[8,128,1024]{1,0,2:T(8,128)(2,1)} %copy.22), calls=%async_computation.1 | async-start | bytes 4194304 | tf_op jit(solution)/shard_map/all_to_all | solution.py:21
  187.9 10.3 %convert_bitcast_fusion = bf16[8,128,1024]{1,2,0:T(8,128)(2,1)S(1)} fusion(bf16[8,1024,1024]{1,2,0:T(8,128)(2,1)} %all-gather.5.cloned.1.call-done, bf16[1024,1024]{1,0:T(8,128)(2,1)} %bitcast.44, s32[]{:T(128)S(6)} %select_n.98, bf16[256,1024]{1,0:T(8,128)(2,1)S(1)} %constant_dynamic-update-slice_fusion, s32[]{:T(128)S(6)} %select_n.97), kind=kOutput, calls=%fused_computation.5 | convolution fusion | flops 2149056512 | bytes 19398664 | tf_op jit(solution)/shard_map/lm,pms->pls/dot_general | solution.py:37
  201.0 6.7 %all-to-all-start = ((bf16[8,128,1024]{1,0,2:T(8,128)(2,1)}), bf16[8,128,1024]{1,0,2:T(8,128)(2,1)}, u32[]{:S(2)}, u32[]{:S(2)}) async-start(bf16[8,128,1024]{1,0,2:T(8,128)(2,1)} %copy.20), calls=%async_computation | async-start | bytes 4194304 | tf_op jit(solution)/shard_map/all_to_all | solution.py:43
  210.9 5.7 %reshape.161 = bf16[128,8192]{1,0:T(8,128)(2,1)S(1)} reshape(bf16[16,8,128,64]{3,2,1,0:T(8,128)(2,1)} %copy.24) | data formatting | bytes 4194304 | tf_op jit(solution)/shard_map/reshape | solution.py:44
  216.6 12.2 %all-to-all-done = bf16[8,128,1024]{1,0,2:T(8,128)(2,1)} async-done(((bf16[8,128,1024]{1,0,2:T(8,128)(2,1)}), bf16[8,128,1024]{1,0,2:T(8,128)(2,1)}, u32[]{:S(2)}, u32[]{:S(2)}) %all-to-all-start) | async-done | bytes 2097184 | tf_op jit(solution)/shard_map/all_to_all | solution.py:43
  228.7 4.8 %copy.21 = bf16[8,128,16,64]{3,1,0,2:T(8,128)(2,1)} copy(bf16[8,128,16,64]{1,0,3,2:T(8,128)(2,1)} %bitcast.9) | data formatting | bytes 4194304 | tf_op jit(solution)/shard_map/all_to_all | solution.py:43
  233.5 6.6 %reshape.160 = bf16[128,8192]{1,0:T(8,128)(2,1)} reshape(bf16[16,8,128,64]{3,2,1,0:T(8,128)(2,1)} %bitcast.39) | data formatting | bytes 4194304 | tf_op jit(solution)/shard_map/reshape | solution.py:45
  243.1 152.0 %all-reduce.3.cloned.1.call-done = f32[128,128]{1,0:T(8,128)} async-done(((f32[128,128]{1,0:T(8,128)}), f32[128,128]{1,0:T(8,128)}) %all-reduce.3.cloned.1.call-update) | async-done | bytes 65552
  (88 shorter events, 35.0 us)
Async XLA Ops:
  6.5 72.7 %all-gather.3.cloned.1.call-start = ((), (), s32[]{:S(2)}) async-start(), calls=%async_computation.2 | async-start | bytes 2113536 | tf_op jit(solution)/shard_map/all_gather | solution.py:22
  7.3 180.6 %all-gather.5.cloned.1.call-start = ((), (), s32[]{:S(2)}) async-start(), calls=%async_computation.3 | async-start | bytes 18874368 | tf_op jit(solution)/shard_map/all_gather | solution.py:40
  10.5 2.3 copy-start.1
  79.2 3.0 copy-start.3
  89.8 0.7 copy-start
  90.6 5.9 %collective-permute-start = (bf16[8,1024]{1,0:T(8,128)(2,1)S(1)}, bf16[8,1024]{1,0:T(8,128)(2,1)S(1)}, u32[]{:S(2)}, u32[]{:S(2)}) collective-permute-start(bf16[8,1024]{1,0:T(8,128)(2,1)S(1)} %copy-done), channel_id=1, source_target_pairs={{0,1},{1,2},{2,3},{3,4},{4,5},{5,6},{6,7},{7,8},{8,9},{9,10},{10,1... | collective-permute-start | bytes 49160 | tf_op jit(solution)/shard_map/ppermute | solution.py:28
  96.5 5.9 %collective-permute-start.1 = (bf16[8,1024]{1,0:T(8,128)(2,1)S(1)}, bf16[8,1024]{1,0:T(8,128)(2,1)S(1)}, u32[]{:S(2)}, u32[]{:S(2)}) collective-permute-start(bf16[8,1024]{1,0:T(8,128)(2,1)S(1)} %collective-permute-done), channel_id=1, source_target_pairs={{0,1},{1,2},{2,3},{3,4},{4,5},{5,6},{6,7},{7,8},{8,9},{9,10},{10,1... | collective-permute-start | bytes 49160 | tf_op jit(solution)/shard_map/ppermute | solution.py:28
  102.4 5.9 %collective-permute-start.2 = (bf16[8,1024]{1,0:T(8,128)(2,1)S(1)}, bf16[8,1024]{1,0:T(8,128)(2,1)S(1)}, u32[]{:S(2)}, u32[]{:S(2)}) collective-permute-start(bf16[8,1024]{1,0:T(8,128)(2,1)S(1)} %collective-permute-done.1), channel_id=1, source_target_pairs={{0,1},{1,2},{2,3},{3,4},{4,5},{5,6},{6,7},{7,8},{8,9},{9,10},{10,1... | collective-permute-start | bytes 49160 | tf_op jit(solution)/shard_map/ppermute | solution.py:28
  108.3 5.9 %collective-permute-start.3 = (bf16[8,1024]{1,0:T(8,128)(2,1)S(1)}, bf16[8,1024]{1,0:T(8,128)(2,1)S(1)}, u32[]{:S(2)}, u32[]{:S(2)}) collective-permute-start(bf16[8,1024]{1,0:T(8,128)(2,1)S(1)} %collective-permute-done.2), channel_id=1, source_target_pairs={{0,1},{1,2},{2,3},{3,4},{4,5},{5,6},{6,7},{7,8},{8,9},{9,10},{10,1... | collective-permute-start | bytes 49160 | tf_op jit(solution)/shard_map/ppermute | solution.py:28
  114.2 5.9 %collective-permute-start.4 = (bf16[8,1024]{1,0:T(8,128)(2,1)S(1)}, bf16[8,1024]{1,0:T(8,128)(2,1)S(1)}, u32[]{:S(2)}, u32[]{:S(2)}) collective-permute-start(bf16[8,1024]{1,0:T(8,128)(2,1)S(1)} %collective-permute-done.3), channel_id=1, source_target_pairs={{0,1},{1,2},{2,3},{3,4},{4,5},{5,6},{6,7},{7,8},{8,9},{9,10},{10,1... | collective-permute-start | bytes 49160 | tf_op jit(solution)/shard_map/ppermute | solution.py:28
  120.1 5.9 %collective-permute-start.5 = (bf16[8,1024]{1,0:T(8,128)(2,1)S(1)}, bf16[8,1024]{1,0:T(8,128)(2,1)S(1)}, u32[]{:S(2)}, u32[]{:S(2)}) collective-permute-start(bf16[8,1024]{1,0:T(8,128)(2,1)S(1)} %collective-permute-done.4), channel_id=1, source_target_pairs={{0,1},{1,2},{2,3},{3,4},{4,5},{5,6},{6,7},{7,8},{8,9},{9,10},{10,1... | collective-permute-start | bytes 49160 | tf_op jit(solution)/shard_map/ppermute | solution.py:28
  126.0 5.9 %collective-permute-start.6 = (bf16[8,1024]{1,0:T(8,128)(2,1)S(1)}, bf16[8,1024]{1,0:T(8,128)(2,1)S(1)}, u32[]{:S(2)}, u32[]{:S(2)}) collective-permute-start(bf16[8,1024]{1,0:T(8,128)(2,1)S(1)} %collective-permute-done.5), channel_id=1, source_target_pairs={{0,1},{1,2},{2,3},{3,4},{4,5},{5,6},{6,7},{7,8},{8,9},{9,10},{10,1... | collective-permute-start | bytes 49160 | tf_op jit(solution)/shard_map/ppermute | solution.py:28
  131.9 5.9 %collective-permute-start.7 = (bf16[8,1024]{1,0:T(8,128)(2,1)S(1)}, bf16[8,1024]{1,0:T(8,128)(2,1)S(1)}, u32[]{:S(2)}, u32[]{:S(2)}) collective-permute-start(bf16[8,1024]{1,0:T(8,128)(2,1)S(1)} %collective-permute-done.6), channel_id=1, source_target_pairs={{0,1},{1,2},{2,3},{3,4},{4,5},{5,6},{6,7},{7,8},{8,9},{9,10},{10,1... | collective-permute-start | bytes 49160 | tf_op jit(solution)/shard_map/ppermute | solution.py:28
  137.8 5.9 %collective-permute-start.8 = (bf16[8,1024]{1,0:T(8,128)(2,1)S(1)}, bf16[8,1024]{1,0:T(8,128)(2,1)S(1)}, u32[]{:S(2)}, u32[]{:S(2)}) collective-permute-start(bf16[8,1024]{1,0:T(8,128)(2,1)S(1)} %collective-permute-done.7), channel_id=1, source_target_pairs={{0,1},{1,2},{2,3},{3,4},{4,5},{5,6},{6,7},{7,8},{8,9},{9,10},{10,1... | collective-permute-start | bytes 49160 | tf_op jit(solution)/shard_map/ppermute | solution.py:28
  143.8 5.9 %collective-permute-start.9 = (bf16[8,1024]{1,0:T(8,128)(2,1)S(1)}, bf16[8,1024]{1,0:T(8,128)(2,1)S(1)}, u32[]{:S(2)}, u32[]{:S(2)}) collective-permute-start(bf16[8,1024]{1,0:T(8,128)(2,1)S(1)} %collective-permute-done.8), channel_id=1, source_target_pairs={{0,1},{1,2},{2,3},{3,4},{4,5},{5,6},{6,7},{7,8},{8,9},{9,10},{10,1... | collective-permute-start | bytes 49160 | tf_op jit(solution)/shard_map/ppermute | solution.py:28
  149.7 5.9 %collective-permute-start.10 = (bf16[8,1024]{1,0:T(8,128)(2,1)S(1)}, bf16[8,1024]{1,0:T(8,128)(2,1)S(1)}, u32[]{:S(2)}, u32[]{:S(2)}) collective-permute-start(bf16[8,1024]{1,0:T(8,128)(2,1)S(1)} %collective-permute-done.9), channel_id=1, source_target_pairs={{0,1},{1,2},{2,3},{3,4},{4,5},{5,6},{6,7},{7,8},{8,9},{9,10},{10,1... | collective-permute-start | bytes 49160 | tf_op jit(solution)/shard_map/ppermute | solution.py:28
  155.6 5.9 %collective-permute-start.11 = (bf16[8,1024]{1,0:T(8,128)(2,1)S(1)}, bf16[8,1024]{1,0:T(8,128)(2,1)S(1)}, u32[]{:S(2)}, u32[]{:S(2)}) collective-permute-start(bf16[8,1024]{1,0:T(8,128)(2,1)S(1)} %collective-permute-done.10), channel_id=1, source_target_pairs={{0,1},{1,2},{2,3},{3,4},{4,5},{5,6},{6,7},{7,8},{8,9},{9,10},{10,1... | collective-permute-start | bytes 49160 | tf_op jit(solution)/shard_map/ppermute | solution.py:28
  161.5 5.9 %collective-permute-start.12 = (bf16[8,1024]{1,0:T(8,128)(2,1)S(1)}, bf16[8,1024]{1,0:T(8,128)(2,1)S(1)}, u32[]{:S(2)}, u32[]{:S(2)}) collective-permute-start(bf16[8,1024]{1,0:T(8,128)(2,1)S(1)} %collective-permute-done.11), channel_id=1, source_target_pairs={{0,1},{1,2},{2,3},{3,4},{4,5},{5,6},{6,7},{7,8},{8,9},{9,10},{10,1... | collective-permute-start | bytes 49160 | tf_op jit(solution)/shard_map/ppermute | solution.py:28
  167.4 5.9 %collective-permute-start.13 = (bf16[8,1024]{1,0:T(8,128)(2,1)S(1)}, bf16[8,1024]{1,0:T(8,128)(2,1)S(1)}, u32[]{:S(2)}, u32[]{:S(2)}) collective-permute-start(bf16[8,1024]{1,0:T(8,128)(2,1)S(1)} %collective-permute-done.12), channel_id=1, source_target_pairs={{0,1},{1,2},{2,3},{3,4},{4,5},{5,6},{6,7},{7,8},{8,9},{9,10},{10,1... | collective-permute-start | bytes 49160 | tf_op jit(solution)/shard_map/ppermute | solution.py:28
  173.3 14.2 %collective-permute-start.14 = (bf16[8,1024]{1,0:T(8,128)(2,1)S(1)}, bf16[8,1024]{1,0:T(8,128)(2,1)S(1)}, u32[]{:S(2)}, u32[]{:S(2)}) collective-permute-start(bf16[8,1024]{1,0:T(8,128)(2,1)S(1)} %collective-permute-done.13), channel_id=1, source_target_pairs={{0,1},{1,2},{2,3},{3,4},{4,5},{5,6},{6,7},{7,8},{8,9},{9,10},{10,1... | collective-permute-start | bytes 49160 | tf_op jit(solution)/shard_map/ppermute | solution.py:28
  176.2 6.3 %copy-start.2 = (s32[8,8]{1,0:T(8,128)S(1)}, s32[8,8]{1,0:T(8,128)}, u32[]{:S(2)}) copy-start(s32[8,8]{1,0:T(8,128)} %param.10) | copy-start | bytes 772
  176.2 24.8 %all-to-all-start.1 = ((bf16[8,128,1024]{1,0,2:T(8,128)(2,1)}), bf16[8,128,1024]{1,0,2:T(8,128)(2,1)S(1)}, u32[]{:S(2)}, u32[]{:S(2)}) async-start(bf16[8,128,1024]{1,0,2:T(8,128)(2,1)} %copy.22), calls=%async_computation.1 | async-start | bytes 4194304 | tf_op jit(solution)/shard_map/all_to_all | solution.py:21
  201.0 27.8 %all-to-all-start = ((bf16[8,128,1024]{1,0,2:T(8,128)(2,1)}), bf16[8,128,1024]{1,0,2:T(8,128)(2,1)}, u32[]{:S(2)}, u32[]{:S(2)}) async-start(bf16[8,128,1024]{1,0,2:T(8,128)(2,1)} %copy.20), calls=%async_computation | async-start | bytes 4194304 | tf_op jit(solution)/shard_map/all_to_all | solution.py:43
  207.7 187.4 %all-reduce.3.cloned.1.call-start = ((), (), s32[]{:S(2)}) async-start(), calls=%async_computation.4 | async-start | bytes 131072
Sparse Core Ops, SparseCore 0:
  10.3 68.8 all-gather.2
  90.0 87.6 all-gather.4
  243.2 151.8 all-reduce.2
